TPU v7x, 256 devices: a whole 4x4x8 slice. The times are simulated.
256 devices in a mesh: seq: 32 (over x, z), chan: 8 (over y, core).
Axes of the slice: x: 4, y: 4, z: 8, core: 2. Of those that a mesh axis runs over, the one named last changes fastest.
Arguments:
- query_rows: bfloat16 [8192, 2048], P('seq', 'chan'), may hold values from -6 to 6
- key_rows: bfloat16 [8192, 2048], P('seq', 'chan'), may hold values from -6 to 6
- value_rows: bfloat16 [8192, 2048], P('seq', 'chan'), may hold values from -6 to 6
- long_filter: float32 [8192, 2048], P('seq', 'chan'), may hold values from -2 to 2
- short_taps: float32 [3, 3, 2048], P(None, None, ('seq', 'chan')), may hold values from -3 to 3
- skip_gain: float32 [2048], P(('seq', 'chan')), may hold values from -3 to 3
- cotangent: bfloat16 [8192, 2048], P('seq', 'chan'), may hold values from -6 to 6
Outputs:
- gated_out: bfloat16 [8192, 2048], P('seq', 'chan')
- query_grad: bfloat16 [8192, 2048], P('seq', 'chan')
- key_grad: bfloat16 [8192, 2048], P('seq', 'chan')
- value_grad: bfloat16 [8192, 2048], P('seq', 'chan')
- filter_grad: float32 [8192, 2048], P('seq', 'chan')
- taps_grad: float32 [3, 3, 2048], P(None, None, 'chan')
- skip_grad: float32 [2048], P('chan')
All inputs are finite; a program needn't handle non-finite values.
Results may differ from a plain program's by a relative error of at most 0.00135.
Values may be sent and summed in bfloat16 or wider, within the bound.
A program may use at most 64 MiB of HBM per device.

v0:
```python
import math
import jax
import jax.numpy as jnp
from jax import lax
from jax.sharding import PartitionSpec as P

exact_dot = lax.Precision.HIGHEST


def from_behind(value, axis, by):
    length = lax.axis_size(axis)
    pairs = [(i, i + by) for i in range(length) if 0 <= i + by < length]
    return lax.ppermute(value, axis, pairs)


def angles(left_index, right_index, period):
    product = left_index[:, None] * right_index[None, :] % period
    return 2.0 * math.pi / period * product.astype(jnp.float32)


def source_transform(pieces, row_start, total):
    sources = pieces.shape[1]
    row_count = pieces.shape[2]
    source_index = jnp.arange(sources, dtype=jnp.int32)
    freq_index = jnp.arange(2 * sources, dtype=jnp.int32)
    theta = angles(source_index, freq_index, 2 * sources)
    real_part = jnp.einsum("fqrc,qk->fkrc", pieces, jnp.cos(theta), precision=exact_dot)
    imag_part = -jnp.einsum("fqrc,qk->fkrc", pieces, jnp.sin(theta), precision=exact_dot)
    row_index = row_start + jnp.arange(row_count, dtype=jnp.int32)
    twist = angles(freq_index, row_index, total)
    cosine = jnp.cos(twist)[None, :, :, None]
    sine = jnp.sin(twist)[None, :, :, None]
    return jnp.stack([real_part * cosine + imag_part * sine, imag_part * cosine - real_part * sine])


def row_transform(spectra, direction):
    length = spectra.shape[3]
    positions = jnp.arange(length, dtype=jnp.int32)
    theta = angles(positions, positions, length)
    cosine = jnp.cos(theta)
    sine = jnp.sin(theta)
    real_cos = jnp.einsum("femc,mk->fekc", spectra[0], cosine, precision=exact_dot)
    real_sin = jnp.einsum("femc,mk->fekc", spectra[0], sine, precision=exact_dot)
    imag_cos = jnp.einsum("femc,mk->fekc", spectra[1], cosine, precision=exact_dot)
    imag_sin = jnp.einsum("femc,mk->fekc", spectra[1], sine, precision=exact_dot)
    return jnp.stack([real_cos - direction * imag_sin, imag_cos + direction * real_sin])


def untwist(spectra, freq_start, total):
    freq_index = freq_start + jnp.arange(spectra.shape[2], dtype=jnp.int32)
    row_index = jnp.arange(spectra.shape[3], dtype=jnp.int32)
    twist = angles(freq_index, row_index, total)
    cosine = jnp.cos(twist)[None, :, :, None]
    sine = jnp.sin(twist)[None, :, :, None]
    return jnp.stack(
        [spectra[0] * cosine - spectra[1] * sine, spectra[1] * cosine + spectra[0] * sine]
    )


def source_sum(spectra, total):
    freqs = spectra.shape[2]
    theta = angles(
        jnp.arange(freqs // 2, dtype=jnp.int32), jnp.arange(freqs, dtype=jnp.int32), freqs
    )
    summed = jnp.einsum("fkrc,qk->fqrc", spectra[0], jnp.cos(theta), precision=exact_dot)
    summed = summed - jnp.einsum("fkrc,qk->fqrc", spectra[1], jnp.sin(theta), precision=exact_dot)
    return summed / total


def spectrum_split(fields):
    devices = lax.axis_size("seq")
    place = lax.axis_index("seq")
    nfields, row_count, channels = fields.shape
    share = row_count // devices
    total = 2 * devices * row_count
    mixed = source_transform(
        lax.all_to_all(
            fields.reshape(nfields, 1, row_count, channels),
            "seq",
            split_axis=2,
            concat_axis=1,
            tiled=True,
        ),
        place * share,
        total,
    )
    mixed = mixed.reshape(2, nfields, devices, 2, share, channels)
    return row_transform(
        lax.all_to_all(mixed, "seq", split_axis=2, concat_axis=4, tiled=True)[:, :, 0], -1.0
    )


def signal_split(spectra):
    devices = lax.axis_size("seq")
    place = lax.axis_index("seq")
    nfields = spectra.shape[1]
    row_count = spectra.shape[3]
    channels = spectra.shape[4]
    share = row_count // devices
    total = 2 * devices * row_count
    turned = untwist(row_transform(spectra, 1.0), 2 * place, total)
    turned = turned.reshape(2, nfields, 1, 2, devices, share, channels)
    pieces = lax.all_to_all(turned, "seq", split_axis=4, concat_axis=2, tiled=True)
    gathered = source_sum(pieces.reshape(2, nfields, 2 * devices, share, pieces.shape[6]), total)
    return lax.all_to_all(gathered, "seq", split_axis=1, concat_axis=2, tiled=True).reshape(
        nfields, row_count, channels
    )


def complex_product(left, right, conjugate):
    right_imag = -right[1] if conjugate else right[1]
    return jnp.stack(
        [left[0] * right[0] - left[1] * right_imag, left[0] * right_imag + left[1] * right[0]]
    )


def per_device(query_rows, key_rows, value_rows, long_filter, short_taps, skip_gain, cotangent):
    row_count, channels = query_rows.shape
    devices = lax.axis_size("seq")
    grad_scale = 1.0 / math.sqrt(row_count * devices)
    all_taps, all_gain = (
        lax.all_gather(short_taps, ("seq", "chan"), axis=2, tiled=True),
        lax.all_gather(skip_gain, ("seq", "chan"), axis=0, tiled=True),
    )
    start = lax.axis_index("chan") * channels
    tap_block = lax.dynamic_slice_in_dim(all_taps, start, channels, 2)
    skip_block = lax.dynamic_slice_in_dim(all_gain, start, channels, 0)
    streams = jnp.stack([query_rows, key_rows, value_rows])
    lower = from_behind(streams[:, row_count - 2 :, :], "seq", 1)
    extended = jnp.concatenate([lower, streams], axis=1).astype(jnp.float32)
    shorted = sum(
        (
            tap_block[:, offset, None, :] * extended[:, 2 - offset : 2 - offset + row_count]
            for offset in range(3)
        )
    )
    query_conv = shorted[0]
    key_conv = shorted[1]
    value_conv = shorted[2]
    product = key_conv * value_conv
    upstream = cotangent.astype(jnp.float32)
    gated_grad = upstream * query_conv
    spectra = spectrum_split(jnp.stack([product, long_filter]))
    prod_spec = spectra[:, 0]
    filt_spec = spectra[:, 1]
    conv_part = signal_split(complex_product(prod_spec, filt_spec, False)[:, None])[0]
    grad_spec = spectrum_split(gated_grad[None])[:, 0]
    back = signal_split(
        jnp.stack(
            [
                complex_product(grad_spec, filt_spec, True),
                complex_product(grad_spec, prod_spec, True),
            ],
            axis=1,
        )
    )
    corr_product = back[0]
    corr_filter = back[1]
    mixed_conv = conv_part + skip_block * product
    gated_out = (query_conv * mixed_conv).astype(jnp.bfloat16)
    query_conv_grad = upstream * mixed_conv
    product_grad = corr_product + skip_block * gated_grad
    filter_grad = grad_scale * corr_filter
    key_conv_grad = product_grad * value_conv
    value_conv_grad = product_grad * key_conv
    conv_grads = jnp.stack([query_conv_grad, key_conv_grad, value_conv_grad])
    upper = from_behind(conv_grads[:, :2, :], "seq", -1)
    ext_grads = jnp.concatenate([conv_grads, upper], axis=1)
    input_grads = sum(
        (
            tap_block[:, offset, None, :] * ext_grads[:, offset : offset + row_count]
            for offset in range(3)
        )
    ).astype(jnp.bfloat16)
    tap_terms = jnp.stack(
        [
            jnp.sum(conv_grads * extended[:, 2 - offset : 2 - offset + row_count], axis=1)
            for offset in range(3)
        ],
        axis=1,
    )
    skip_terms = jnp.sum(gated_grad * product, axis=0)
    tap_total, skip_total = lax.psum((tap_terms, skip_terms), "seq")
    return (
        gated_out,
        input_grads[0],
        input_grads[1],
        input_grads[2],
        filter_grad,
        grad_scale * tap_total,
        grad_scale * skip_total,
    )


def solution(mesh):
    in_specs = (
        P("seq", "chan"),
        P("seq", "chan"),
        P("seq", "chan"),
        P("seq", "chan"),
        P(None, None, ("seq", "chan")),
        P(("seq", "chan")),
        P("seq", "chan"),
    )
    out_specs = (
        P("seq", "chan"),
        P("seq", "chan"),
        P("seq", "chan"),
        P("seq", "chan"),
        P("seq", "chan"),
        P(None, None, "chan"),
        P("chan"),
    )
    return jax.shard_map(
        per_device, mesh=mesh, in_specs=in_specs, out_specs=out_specs, check_vma=False
    )
```

profile of v0, /device:TPU:8, one launch (start us, length us, event | category | flops | bytes accessed | tf_op | source)
XLA Modules:
  0.0 597.0 jit_solution(4957405621104877456)
XLA Ops:
  1.4 3.8 collective-permute-start
  6.0 83.8 %all_gather.6 = f32[3,3,2048]{1,0,2:T(4,128)} all-gather(f32[3,3,8]{1,0,2:T(4,128)S(1)} %copy.38), channel_id=1, replica_groups=mesh['seq'=32,'chan'=8] {'seq','chan'}, dimensions={2}, use_global_device_ids=true | all-gather | bytes 74016 | tf_op jit(solution)/shard_map/all_gather | solution.py:122
  89.7 2.1 constant_dynamic-slice_fusion.1
  94.4 7.2 %all-to-all-start.4 = ((f32[1,1,256,256]{3,1,0,2:T(1,128)}), f32[1,1,256,256]{3,1,0,2:T(1,128)S(1)}, u32[]{:S(2)}, u32[]{:S(2)}) async-start(f32[1,1,256,256]{3,1,0,2:T(1,128)} %copy.55), calls=%async_computation.4 | async-start | bytes 524288 | tf_op jit(solution)/shard_map/all_to_all | solution.py:77
  102.9 11.3 %all-to-all-done.4 = f32[1,1,256,256]{3,1,0,2:T(1,128)S(1)} async-done(((f32[1,1,256,256]{3,1,0,2:T(1,128)}), f32[1,1,256,256]{3,1,0,2:T(1,128)S(1)}, u32[]{:S(2)}, u32[]{:S(2)}) %all-to-all-start.4) | async-done | bytes 262176 | tf_op jit(solution)/shard_map/all_to_all | solution.py:77
  114.3 4.7 all-to-all-start
  121.8 1.6 copy.78
  123.4 12.5 %all-to-all-done = f32[2,1,256,256]{3,0,1,2:T(2,128)S(1)} async-done(((f32[2,1,256,256]{3,0,1,2:T(2,128)}), f32[2,1,256,256]{3,0,1,2:T(2,128)S(1)}, u32[]{:S(2)}, u32[]{:S(2)}) %all-to-all-start) | async-done | bytes 524320 | tf_op jit(solution)/shard_map/all_to_all | solution.py:77
  135.9 5.8 all-to-all-start.5
  144.2 1.6 stack.117
  145.8 1.6 stack.118
  147.4 2.7 pad_maximum_fusion
  150.1 2.5 copy.74
  152.7 17.1 %all-to-all-done.5 = f32[2,1,32,2,8,256]{5,3,4,1,0,2:T(2,128)} async-done(((f32[2,1,32,2,8,256]{5,3,4,1,0,2:T(2,128)}), f32[2,1,32,2,8,256]{5,3,4,1,0,2:T(2,128)}, u32[]{:S(2)}, u32[]{:S(2)}) %all-to-all-start.5) | async-done | bytes 1048608 | tf_op jit(solution)/shard_map/all_to_all | solution.py:89
  169.8 4.9 all-to-all-start.1
  174.8 2.4 fusion.254
  177.2 47.1 %all-to-all-done.1 = f32[2,2,32,2,8,256]{5,3,4,1,0,2:T(2,128)S(1)} async-done(((f32[2,2,32,2,8,256]{5,3,4,1,0,2:T(2,128)}), f32[2,2,32,2,8,256]{5,3,4,1,0,2:T(2,128)S(1)}, u32[]{:S(2)}, u32[]{:S(2)}) %all-to-all-start.1) | async-done | bytes 2097184 | tf_op jit(solution)/shard_map/all_to_all | solution.py:89
  225.2 2.0 fusion.23
  227.2 2.0 fusion.19
  229.2 2.1 fusion.5
  231.3 2.1 fusion.3
  233.6 1.6 fusion.45
  235.2 13.2 %fusion.49 = f32[256,2,256]{2,0,1:T(8,128)S(1)} fusion(f32[1,1,2,256,256]{4,3,2,1,0:T(8,128)S(1)} %get-tuple-element.40), kind=kOutput, calls=%fused_computation.91 | convolution fusion | flops 403570688 | bytes 1048576 | tf_op jit(solution)/shard_map/femc,mk->fekc/dot_general | solution.py:42
  248.4 1.6 fusion.12
  250.1 1.8 subtract_bitcast_fusion.2
  253.1 6.2 %all-to-all-start.2 = ((f32[2,1,1,2,32,8,256]{6,5,3,2,1,0,4:T(8,128)}), f32[2,1,1,2,32,8,256]{6,5,3,2,1,0,4:T(8,128)}, u32[]{:S(2)}, u32[]{:S(2)}) async-start(f32[2,1,1,2,32,8,256]{6,5,3,2,1,0,4:T(8,128)} %copy.75), calls=%async_computation.2 | async-start | bytes 2097152 | tf_op jit(solution)/shard_map/all_to_all | solution.py:103
  259.2 1.6 fusion.40
  260.9 2.7 fusion.11
  263.6 1.6 fusion.36
  265.2 2.0 fusion.32
  267.3 2.0 fusion.58
  269.4 2.0 fusion.79
  271.4 2.3 fusion
  273.7 2.3 subtract_bitcast_fusion
  276.2 1.6 copy.79
  277.8 9.7 %all-to-all-done.2 = f32[2,1,1,2,32,8,256]{6,5,3,2,1,0,4:T(8,128)} async-done(((f32[2,1,1,2,32,8,256]{6,5,3,2,1,0,4:T(8,128)}), f32[2,1,1,2,32,8,256]{6,5,3,2,1,0,4:T(8,128)}, u32[]{:S(2)}, u32[]{:S(2)}) %all-to-all-start.2) | async-done | bytes 1048608 | tf_op jit(solution)/shard_map/all_to_all | solution.py:103
  287.5 4.9 all-to-all-start.6
  295.7 46.4 %all-to-all-done.6 = f32[2,2,1,2,32,8,256]{6,5,3,1,2,0,4:T(8,128)S(1)} async-done(((f32[2,2,1,2,32,8,256]{6,5,3,1,2,0,4:T(8,128)}), f32[2,2,1,2,32,8,256]{6,5,3,1,2,0,4:T(8,128)S(1)}, u32[]{:S(2)}, u32[]{:S(2)}) %all-to-all-start.6) | async-done | bytes 2097184 | tf_op jit(solution)/shard_map/all_to_all | solution.py:103
  342.1 6.0 %all-to-all-start.3 = ((f32[1,32,8,256]{3,2,0,1:T(8,128)}), f32[1,32,8,256]{3,2,0,1:T(8,128)S(1)}, u32[]{:S(2)}, u32[]{:S(2)}) async-start(f32[1,32,8,256]{3,2,0,1:T(8,128)} %copy.54), calls=%async_computation.3 | async-start | bytes 524288 | tf_op jit(solution)/shard_map/all_to_all | solution.py:105
  349.3 1.5 copy.65
  350.8 1.9 squeeze.40
  352.7 2.7 copy.64
  355.4 2.9 squeeze.39
  358.4 1.9 fusion.118
  362.2 9.8 %all-to-all-start.7 = ((f32[2,32,8,256]{3,2,0,1:T(8,128)}), f32[2,32,8,256]{3,2,0,1:T(8,128)S(1)}, u32[]{:S(2)}, u32[]{:S(2)}) async-start(f32[2,32,8,256]{3,2,0,1:T(8,128)} %copy.66), calls=%async_computation.7 | async-start | bytes 1048576 | tf_op jit(solution)/shard_map/all_to_all | solution.py:105
  372.3 75.6 %all-reduce = f32[2048]{0:T(1024)S(1)} all-reduce(f32[2048]{0:T(1024)S(1)} %dynamic-update-slice), channel_id=1, replica_groups=mesh['seq'=32,'chan'=8] {'seq','chan'}, use_global_device_ids=true, to_apply=%add | all-reduce | flops 2048 | bytes 16384
  450.8 3.5 collective-permute-done.1
  454.9 139.8 %all-reduce.1 = (f32[3,3,256]{2,0,1:T(4,128)S(1)}, f32[256]{0:T(256)S(1)}) all-reduce(f32[3,3,256]{2,0,1:T(4,128)S(1)} %pad_maximum_fusion.7, f32[256]{0:T(256)S(1)} %get-tuple-element.57), channel_id=1, replica_groups=mesh['seq'=32,'chan'=8] {'seq'}, use_global_device_ids=true, to_apply=%region_3.4 | all-reduce | flops 2560 | bytes 20480 | tf_op jit(solution)/shard_map/psum | solution.py:183
  (78 shorter events, 25.2 us)
Async XLA Ops:
  1.4 91.1 %collective-permute-start = (bf16[3,2,256]{2,1,0:T(2,128)(2,1)S(1)}, bf16[3,2,256]{2,1,0:T(2,128)(2,1)S(1)}, u32[]{:S(2)}, u32[]{:S(2)}) collective-permute-start(bf16[3,2,256]{2,1,0:T(2,128)(2,1)S(1)} %pad_maximum_fusion.8), channel_id=1, source_target_pairs={{0,8},{8,16},{16,24},{24,32},{32,40},{40,48},{48,56},{56,64},{64,7... | collective-permute-start | bytes 9224 | tf_op jit(solution)/shard_map/ppermute | solution.py:13
  89.7 2.7 copy-start.4
  89.7 2.7 copy-start.5
  89.7 2.8 copy-start.6
  92.5 0.9 copy-start.7
  92.6 9.1 %copy-start.9 = (f32[256,256]{1,0:T(8,128)S(1)}, f32[256,256]{1,0:T(8,128)}, u32[]{:S(2)}) copy-start(f32[256,256]{1,0:T(8,128)} %param.10) | copy-start | bytes 786436
  93.4 9.5 %copy-start = (f32[3,256,256]{2,1,0:T(8,128)}, f32[3,256,256]{2,1,0:T(8,128)S(1)}, u32[]{:S(2)}) copy-start(f32[3,256,256]{2,1,0:T(8,128)S(1)} %multiply_add_fusion) | copy-start | bytes 2359300
  94.4 19.9 %all-to-all-start.4 = ((f32[1,1,256,256]{3,1,0,2:T(1,128)}), f32[1,1,256,256]{3,1,0,2:T(1,128)S(1)}, u32[]{:S(2)}, u32[]{:S(2)}) async-start(f32[1,1,256,256]{3,1,0,2:T(1,128)} %copy.55), calls=%async_computation.4 | async-start | bytes 524288 | tf_op jit(solution)/shard_map/all_to_all | solution.py:77
  114.3 21.6 %all-to-all-start = ((f32[2,1,256,256]{3,0,1,2:T(2,128)}), f32[2,1,256,256]{3,0,1,2:T(2,128)S(1)}, u32[]{:S(2)}, u32[]{:S(2)}) async-start(f32[2,1,256,256]{3,0,1,2:T(2,128)} %copy.42), calls=%async_computation | async-start | bytes 1048576 | tf_op jit(solution)/shard_map/all_to_all | solution.py:77
  135.9 33.9 %all-to-all-start.5 = ((f32[2,1,32,2,8,256]{5,3,4,1,0,2:T(2,128)}), f32[2,1,32,2,8,256]{5,3,4,1,0,2:T(2,128)}, u32[]{:S(2)}, u32[]{:S(2)}) async-start(f32[2,1,32,2,8,256]{5,3,4,1,0,2:T(2,128)} %copy.78), calls=%async_computation.5 | async-start | bytes 2097152 | tf_op jit(solution)/shard_map/all_to_all | solution.py:89
  145.8 1.6 copy-start.2
  169.8 54.5 %all-to-all-start.1 = ((f32[2,2,32,2,8,256]{5,3,4,1,0,2:T(2,128)}), f32[2,2,32,2,8,256]{5,3,4,1,0,2:T(2,128)S(1)}, u32[]{:S(2)}, u32[]{:S(2)}) async-start(f32[2,2,32,2,8,256]{5,3,4,1,0,2:T(2,128)} %copy.74), calls=%async_computation.1 | async-start | bytes 4194304 | tf_op jit(solution)/shard_map/all_to_all | solution.py:89
  253.1 34.5 %all-to-all-start.2 = ((f32[2,1,1,2,32,8,256]{6,5,3,2,1,0,4:T(8,128)}), f32[2,1,1,2,32,8,256]{6,5,3,2,1,0,4:T(8,128)}, u32[]{:S(2)}, u32[]{:S(2)}) async-start(f32[2,1,1,2,32,8,256]{6,5,3,2,1,0,4:T(8,128)} %copy.75), calls=%async_computation.2 | async-start | bytes 2097152 | tf_op jit(solution)/shard_map/all_to_all | solution.py:103
  259.2 4.3 copy-start.3
  287.5 54.6 %all-to-all-start.6 = ((f32[2,2,1,2,32,8,256]{6,5,3,1,2,0,4:T(8,128)}), f32[2,2,1,2,32,8,256]{6,5,3,1,2,0,4:T(8,128)S(1)}, u32[]{:S(2)}, u32[]{:S(2)}) async-start(f32[2,2,1,2,32,8,256]{6,5,3,1,2,0,4:T(8,128)} %copy.79), calls=%async_computation.6 | async-start | bytes 4194304 | tf_op jit(solution)/shard_map/all_to_all | solution.py:103
  342.1 20.1 %all-to-all-start.3 = ((f32[1,32,8,256]{3,2,0,1:T(8,128)}), f32[1,32,8,256]{3,2,0,1:T(8,128)S(1)}, u32[]{:S(2)}, u32[]{:S(2)}) async-start(f32[1,32,8,256]{3,2,0,1:T(8,128)} %copy.54), calls=%async_computation.3 | async-start | bytes 524288 | tf_op jit(solution)/shard_map/all_to_all | solution.py:105
  360.3 11.7 %copy-start.10 = (f32[8]{0:T(128)S(1)}, f32[8]{0:T(128)}, u32[]{:S(2)}) copy-start(f32[8]{0:T(128)} %param.12) | copy-start | bytes 100
  360.3 87.6 %copy-start.1 = (f32[3,256,256]{2,1,0:T(8,128)S(1)}, f32[3,256,256]{2,1,0:T(8,128)}, u32[]{:S(2)}) copy-start(f32[3,256,256]{2,1,0:T(8,128)} %copy-done) | copy-start | bytes 2359300
  360.3 87.6 %copy-start.8 = (bf16[256,256]{1,0:T(8,128)(2,1)S(1)}, bf16[256,256]{1,0:T(8,128)(2,1)}, u32[]{:S(2)}) copy-start(bf16[256,256]{1,0:T(8,128)(2,1)} %param.13) | copy-start | bytes 393220
  362.2 85.8 %all-to-all-start.7 = ((f32[2,32,8,256]{3,2,0,1:T(8,128)}), f32[2,32,8,256]{3,2,0,1:T(8,128)S(1)}, u32[]{:S(2)}, u32[]{:S(2)}) async-start(f32[2,32,8,256]{3,2,0,1:T(8,128)} %copy.66), calls=%async_computation.7 | async-start | bytes 1048576 | tf_op jit(solution)/shard_map/all_to_all | solution.py:105
  448.8 5.5 collective-permute-start.1
where the time goes:
time: 606 us; the launch traced here: 597 us
  blocking collectives  299 us (49%)
  waiting for transfers between devices  148 us (24%)
  starting transfers between devices  54.5 us (9%)
  matrix products  50.8 us (8%)
  local copies, waits for them, and re-layouts  35.4 us (6%)
  other arithmetic  7.9 us (1%)
    psum x1, blocking collectives, per_device(): tap_total, skip_total = lax.psum((tap_terms, skip_terms), 'seq')  140 us
    all_gather x1, blocking collectives, per_device(): lax.all_gather(short_taps, ('seq', 'chan'), axis=2, tiled=True)  83.8 us
    unnamed x1, blocking collectives  75.6 us
    all_to_all x2, waiting for transfers between devices, spectrum_split(): lax.all_to_all(mixed, 'seq', split_axis=2, concat_axis=4, tiled=True)  64.2 us
    all_to_all x2, waiting for transfers between devices, signal_split(): lax.all_to_all(turned, 'seq', split_axis=4, concat_axis=2, tiled=True)  56.1 us
    all_to_all x2, waiting for transfers between devices, spectrum_split(): lax.all_to_all(fields.reshape(nfields, 1, row_count, channels), 'seq', sp...  23.8 us
    dot_general x4, matrix products, row_transform(): jnp.einsum('femc,mk->fekc', spectra[0], cosine, precision=exact_dot)  18.9 us
    all_to_all x2, starting transfers between devices, signal_split(): lax.all_to_all(gathered, 'seq', split_axis=1, concat_axis=2, tiled=True)  15.8 us
  transfers between devices with their start and end apart: 10, of which 7 were waited for; matrix products, arithmetic and copies ran while one was open for 10% of the time, Pallas kernels for 0%

commit v1 on v0

--- a/solution.py
+++ b/solution.py
@@ -100,7 +100,10 @@
     total = 2 * devices * row_count
     turned = untwist(row_transform(spectra, 1.0), 2 * place, total)
     turned = turned.reshape(2, nfields, 1, 2, devices, share, channels)
-    pieces = lax.all_to_all(turned, "seq", split_axis=4, concat_axis=2, tiled=True)
+    pieces = jnp.concatenate(
+        lax.all_to_all(jnp.stack(jnp.split(turned, lax.axis_size("seq"), axis=4)), "seq", 0, 0),
+        axis=2,
+    )
     gathered = source_sum(pieces.reshape(2, nfields, 2 * devices, share, pieces.shape[6]), total)
     return lax.all_to_all(gathered, "seq", split_axis=1, concat_axis=2, tiled=True).reshape(
         nfields, row_count, channels

time: 606 us -> 631 us (1.041)
  other arithmetic: 7.9 us -> 27.2 us
    unnamed x0 -> x62, other arithmetic: none -> 18.9 us
    all_to_all x2, waiting for transfers between devices: 56.1 us -> 67.1 us  [signal_split(): lax.all_to_all(jnp.stack(jnp.split(turned, lax.axis_size('seq'), axis=4))...]
    dot_general x4, matrix products: 18.9 us -> 8.29 us  [row_transform(): jnp.einsum('femc,mk->fekc', spectra[0], cosine, precision=exact_dot)]
    dot_general x4, matrix products: 8.88 us -> 16.6 us  [row_transform(): jnp.einsum('femc,mk->fekc', spectra[1], sine, precision=exact_dot)]
  transfers between devices with their start and end apart: 10 -> 10, of which waited for: 7 -> 7; matrix products, arithmetic and copies ran while one was open for 10% -> 8% of each run, Pallas kernels for 0% -> 0%
where the time goes in v1:
time: 631 us; the launch traced here: 622 us
  blocking collectives  299 us (47%)
  waiting for transfers between devices  154 us (24%)
  starting transfers between devices  54.5 us (9%)
  matrix products  51 us (8%)
  local copies, waits for them, and re-layouts  34.3 us (5%)
  other arithmetic  27.2 us (4%)
    psum x1, blocking collectives, per_device(): tap_total, skip_total = lax.psum((tap_terms, skip_terms), 'seq')  140 us
    all_gather x1, blocking collectives, per_device(): lax.all_gather(short_taps, ('seq', 'chan'), axis=2, tiled=True)  83.8 us
    unnamed x1, blocking collectives  75.6 us
    all_to_all x2, waiting for transfers between devices, signal_split(): lax.all_to_all(jnp.stack(jnp.split(turned, lax.axis_size('seq'), axis=4))...  67.1 us
    all_to_all x2, waiting for transfers between devices, spectrum_split(): lax.all_to_all(mixed, 'seq', split_axis=2, concat_axis=4, tiled=True)  59.5 us
    all_to_all x2, waiting for transfers between devices, spectrum_split(): lax.all_to_all(fields.reshape(nfields, 1, row_count, channels), 'seq', sp...  24 us
    unnamed x62, other arithmetic  18.9 us
    dot_general x4, matrix products, row_transform(): jnp.einsum('femc,mk->fekc', spectra[1], sine, precision=exact_dot)  16.6 us
  transfers between devices with their start and end apart: 10, of which 7 were waited for; matrix products, arithmetic and copies ran while one was open for 8% of the time, Pallas kernels for 0%

profile of v1, /device:TPU:8, one launch (start us, length us, event | category | flops | bytes accessed | tf_op | source)
XLA Modules:
  0.0 622.1 jit_solution(16646387764482466665)
XLA Ops:
  1.4 3.8 collective-permute-start
  6.0 83.8 %all_gather.6 = f32[3,3,2048]{1,0,2:T(4,128)} all-gather(f32[3,3,8]{1,0,2:T(4,128)S(1)} %copy.162), channel_id=1, replica_groups=mesh['seq'=32,'chan'=8] {'seq','chan'}, dimensions={2}, use_global_device_ids=true | all-gather | bytes 74016 | tf_op jit(solution)/shard_map/all_gather | solution.py:125
  89.8 2.2 constant_dynamic-slice_fusion.1
  94.5 7.1 %all-to-all-start.4 = ((f32[1,1,256,256]{3,1,0,2:T(1,128)}), f32[1,1,256,256]{3,1,0,2:T(1,128)S(1)}, u32[]{:S(2)}, u32[]{:S(2)}) async-start(f32[1,1,256,256]{3,1,0,2:T(1,128)} %copy.208), calls=%async_computation.4 | async-start | bytes 524288 | tf_op jit(solution)/shard_map/all_to_all | solution.py:77
  103.0 11.5 %all-to-all-done.4 = f32[1,1,256,256]{3,1,0,2:T(1,128)S(1)} async-done(((f32[1,1,256,256]{3,1,0,2:T(1,128)}), f32[1,1,256,256]{3,1,0,2:T(1,128)S(1)}, u32[]{:S(2)}, u32[]{:S(2)}) %all-to-all-start.4) | async-done | bytes 262176 | tf_op jit(solution)/shard_map/all_to_all | solution.py:77
  114.4 4.5 all-to-all-start
  121.8 1.6 copy.259
  123.4 12.5 %all-to-all-done = f32[2,1,256,256]{3,0,1,2:T(2,128)S(1)} async-done(((f32[2,1,256,256]{3,0,1,2:T(2,128)}), f32[2,1,256,256]{3,0,1,2:T(2,128)S(1)}, u32[]{:S(2)}, u32[]{:S(2)}) %all-to-all-start) | async-done | bytes 524320 | tf_op jit(solution)/shard_map/all_to_all | solution.py:77
  135.9 5.7 all-to-all-start.5
  142.7 1.4 add_bitcast_fusion.1
  144.1 1.6 stack.315
  145.7 1.6 stack.316
  147.3 2.7 pad_maximum_fusion
  150.1 2.6 copy.256
  152.6 17.3 %all-to-all-done.5 = f32[2,1,32,2,8,256]{5,3,4,1,0,2:T(2,128)} async-done(((f32[2,1,32,2,8,256]{5,3,4,1,0,2:T(2,128)}), f32[2,1,32,2,8,256]{5,3,4,1,0,2:T(2,128)}, u32[]{:S(2)}, u32[]{:S(2)}) %all-to-all-start.5) | async-done | bytes 1048608 | tf_op jit(solution)/shard_map/all_to_all | solution.py:89
  169.9 4.9 all-to-all-start.1
  174.9 1.6 fusion.318
  176.5 1.6 fusion.40
  178.2 1.6 fusion.11
  179.8 2.4 fusion.36
  182.3 42.2 %all-to-all-done.1 = f32[2,2,32,2,8,256]{5,3,4,1,0,2:T(2,128)S(1)} async-done(((f32[2,2,32,2,8,256]{5,3,4,1,0,2:T(2,128)}), f32[2,2,32,2,8,256]{5,3,4,1,0,2:T(2,128)S(1)}, u32[]{:S(2)}, u32[]{:S(2)}) %all-to-all-start.1) | async-done | bytes 2097184 | tf_op jit(solution)/shard_map/all_to_all | solution.py:89
  225.3 2.0 fusion.23
  227.3 2.0 fusion.19
  229.4 10.8 %fusion.5 = f32[1,2,2,256,256]{4,3,2,1,0:T(8,128)S(1)} fusion(f32[256,2,2,256]{3,0,2,1:T(8,128)S(1)} %fusion.23, f32[1,2,1,2,32,8,256]{6,3,5,1,0,4,2:T(2,128)S(1)} %get-tuple-element.42), kind=kOutput, calls=%fused_computation.137 | convolution fusion | flops 806748160 | bytes 3145728 | tf_op jit(solution)/shard_map/femc,mk->fekc/dot_general | solution.py:45
  240.2 2.1 fusion.3
  243.5 2.0 fusion.32
  245.6 3.0 fusion.58
  248.6 3.0 fusion.79
  251.6 1.6 fusion.45
  253.3 1.6 fusion.49
  254.9 1.8 fusion.12
  256.8 1.8 subtract_bitcast_fusion.2
  277.9 6.1 all-to-all-start.2
  284.1 3.4 fusion
  287.4 2.3 subtract_bitcast_fusion
  291.6 20.7 %all-to-all-done.2 = f32[32,2,1,1,2,1,8,256]{7,6,4,1,5,3,2,0:T(8,128)} async-done(((f32[32,2,1,1,2,1,8,256]{7,6,4,1,5,3,2,0:T(8,128)}), f32[32,2,1,1,2,1,8,256]{7,6,4,1,5,3,2,0:T(8,128)}, u32[]{:S(2)}, u32[]{:S(2)}) %all-to-all-start.2) | async-done | bytes 1048608 | tf_op jit(solution)/shard_map/all_to_all | solution.py:104
  312.3 4.9 all-to-all-start.6
  320.5 46.4 %all-to-all-done.6 = f32[32,2,2,1,2,1,8,256]{7,6,4,2,1,5,3,0:T(8,128)S(1)} async-done(((f32[32,2,2,1,2,1,8,256]{7,6,4,2,1,5,3,0:T(8,128)}), f32[32,2,2,1,2,1,8,256]{7,6,4,2,1,5,3,0:T(8,128)S(1)}, u32[]{:S(2)}, u32[]{:S(2)}) %all-to-all-start.6) | async-done | bytes 2097184 | tf_op jit(solution)/shard_map/all_to_all | solution.py:104
  366.9 6.3 %all-to-all-start.3 = ((f32[1,32,8,256]{3,2,0,1:T(8,128)}), f32[1,32,8,256]{3,2,0,1:T(8,128)S(1)}, u32[]{:S(2)}, u32[]{:S(2)}) async-start(f32[1,32,8,256]{3,2,0,1:T(8,128)} %copy.207), calls=%async_computation.3 | async-start | bytes 524288 | tf_op jit(solution)/shard_map/all_to_all | solution.py:108
  374.3 1.5 copy.247
  375.9 1.9 squeeze.40
  377.8 2.7 copy.246
  380.5 2.9 squeeze.39
  383.5 1.9 fusion.182
  387.2 9.9 %all-to-all-start.7 = ((f32[2,32,8,256]{3,2,0,1:T(8,128)}), f32[2,32,8,256]{3,2,0,1:T(8,128)S(1)}, u32[]{:S(2)}, u32[]{:S(2)}) async-start(f32[2,32,8,256]{3,2,0,1:T(8,128)} %copy.248), calls=%async_computation.7 | async-start | bytes 1048576 | tf_op jit(solution)/shard_map/all_to_all | solution.py:108
  397.4 75.6 %all-reduce = f32[2048]{0:T(1024)S(1)} all-reduce(f32[2048]{0:T(1024)S(1)} %dynamic-update-slice), channel_id=1, replica_groups=mesh['seq'=32,'chan'=8] {'seq','chan'}, use_global_device_ids=true, to_apply=%add | all-reduce | flops 2048 | bytes 16384
  476.0 3.5 collective-permute-done.1
  480.1 139.6 %all-reduce.1 = (f32[3,3,256]{2,0,1:T(4,128)S(1)}, f32[256]{0:T(256)S(1)}) all-reduce(f32[3,3,256]{2,0,1:T(4,128)S(1)} %pad_maximum_fusion.7, f32[256]{0:T(256)S(1)} %get-tuple-element.57), channel_id=1, replica_groups=mesh['seq'=32,'chan'=8] {'seq'}, use_global_device_ids=true, to_apply=%region_3.4 | all-reduce | flops 2560 | bytes 20480 | tf_op jit(solution)/shard_map/psum | solution.py:186
  (146 shorter events, 44.4 us)
Async XLA Ops:
  1.4 91.2 %collective-permute-start = (bf16[3,2,256]{2,1,0:T(2,128)(2,1)S(1)}, bf16[3,2,256]{2,1,0:T(2,128)(2,1)S(1)}, u32[]{:S(2)}, u32[]{:S(2)}) collective-permute-start(bf16[3,2,256]{2,1,0:T(2,128)(2,1)S(1)} %pad_maximum_fusion.8), channel_id=1, source_target_pairs={{0,8},{8,16},{16,24},{24,32},{32,40},{40,48},{48,56},{56,64},{64,7... | collective-permute-start | bytes 9224 | tf_op jit(solution)/shard_map/ppermute | solution.py:13
  89.8 2.8 copy-start.8
  89.8 2.8 copy-start.9
  89.8 2.8 copy-start.10
  92.6 0.9 copy-start.11
  92.7 9.0 %copy-start.13 = (f32[256,256]{1,0:T(8,128)S(1)}, f32[256,256]{1,0:T(8,128)}, u32[]{:S(2)}) copy-start(f32[256,256]{1,0:T(8,128)} %param.10) | copy-start | bytes 786436
  93.5 9.5 %copy-start = (f32[3,256,256]{2,1,0:T(8,128)}, f32[3,256,256]{2,1,0:T(8,128)S(1)}, u32[]{:S(2)}) copy-start(f32[3,256,256]{2,1,0:T(8,128)S(1)} %multiply_add_fusion) | copy-start | bytes 2359300
  94.5 19.9 %all-to-all-start.4 = ((f32[1,1,256,256]{3,1,0,2:T(1,128)}), f32[1,1,256,256]{3,1,0,2:T(1,128)S(1)}, u32[]{:S(2)}, u32[]{:S(2)}) async-start(f32[1,1,256,256]{3,1,0,2:T(1,128)} %copy.208), calls=%async_computation.4 | async-start | bytes 524288 | tf_op jit(solution)/shard_map/all_to_all | solution.py:77
  114.4 21.5 %all-to-all-start = ((f32[2,1,256,256]{3,0,1,2:T(2,128)}), f32[2,1,256,256]{3,0,1,2:T(2,128)S(1)}, u32[]{:S(2)}, u32[]{:S(2)}) async-start(f32[2,1,256,256]{3,0,1,2:T(2,128)} %copy.166), calls=%async_computation | async-start | bytes 1048576 | tf_op jit(solution)/shard_map/all_to_all | solution.py:77
  135.9 34.0 %all-to-all-start.5 = ((f32[2,1,32,2,8,256]{5,3,4,1,0,2:T(2,128)}), f32[2,1,32,2,8,256]{5,3,4,1,0,2:T(2,128)}, u32[]{:S(2)}, u32[]{:S(2)}) async-start(f32[2,1,32,2,8,256]{5,3,4,1,0,2:T(2,128)} %copy.259), calls=%async_computation.5 | async-start | bytes 2097152 | tf_op jit(solution)/shard_map/all_to_all | solution.py:89
  145.7 1.6 copy-start.3
  169.9 54.6 %all-to-all-start.1 = ((f32[2,2,32,2,8,256]{5,3,4,1,0,2:T(2,128)}), f32[2,2,32,2,8,256]{5,3,4,1,0,2:T(2,128)S(1)}, u32[]{:S(2)}, u32[]{:S(2)}) async-start(f32[2,2,32,2,8,256]{5,3,4,1,0,2:T(2,128)} %copy.256), calls=%async_computation.1 | async-start | bytes 4194304 | tf_op jit(solution)/shard_map/all_to_all | solution.py:89
  176.5 3.3 copy-start.5
  242.3 1.0 copy-start.6
  242.3 1.2 copy-start.7
  277.9 34.4 %all-to-all-start.2 = ((f32[32,2,1,1,2,1,8,256]{7,6,4,1,5,3,2,0:T(8,128)}), f32[32,2,1,1,2,1,8,256]{7,6,4,1,5,3,2,0:T(8,128)}, u32[]{:S(2)}, u32[]{:S(2)}) async-start(f32[32,2,1,1,2,1,8,256]{7,6,4,1,5,3,2,0:T(8,128)} %constant_dynamic-update-slice_fusion), calls=%async_computation.2 | async-start | bytes 2097152 | tf_op jit(solution)/shard_map/all_to_all | solution.py:104
  284.1 3.4 copy-start.2
  290.2 1.4 copy-start.4
  312.3 54.6 %all-to-all-start.6 = ((f32[32,2,2,1,2,1,8,256]{7,6,4,2,1,5,3,0:T(8,128)}), f32[32,2,2,1,2,1,8,256]{7,6,4,2,1,5,3,0:T(8,128)S(1)}, u32[]{:S(2)}, u32[]{:S(2)}) async-start(f32[32,2,2,1,2,1,8,256]{7,6,4,2,1,5,3,0:T(8,128)} %copy-done.4), calls=%async_computation.6 | async-start | bytes 4194304 | tf_op jit(solution)/shard_map/all_to_all | solution.py:104
  366.9 20.3 %all-to-all-start.3 = ((f32[1,32,8,256]{3,2,0,1:T(8,128)}), f32[1,32,8,256]{3,2,0,1:T(8,128)S(1)}, u32[]{:S(2)}, u32[]{:S(2)}) async-start(f32[1,32,8,256]{3,2,0,1:T(8,128)} %copy.207), calls=%async_computation.3 | async-start | bytes 524288 | tf_op jit(solution)/shard_map/all_to_all | solution.py:108
  385.4 11.8 %copy-start.14 = (f32[8]{0:T(128)S(1)}, f32[8]{0:T(128)}, u32[]{:S(2)}) copy-start(f32[8]{0:T(128)} %param.12) | copy-start | bytes 100
  385.4 87.7 %copy-start.1 = (f32[3,256,256]{2,1,0:T(8,128)S(1)}, f32[3,256,256]{2,1,0:T(8,128)}, u32[]{:S(2)}) copy-start(f32[3,256,256]{2,1,0:T(8,128)} %copy-done) | copy-start | bytes 2359300
  385.4 87.7 %copy-start.12 = (bf16[256,256]{1,0:T(8,128)(2,1)S(1)}, bf16[256,256]{1,0:T(8,128)(2,1)}, u32[]{:S(2)}) copy-start(bf16[256,256]{1,0:T(8,128)(2,1)} %param.13) | copy-start | bytes 393220
  387.2 85.9 %all-to-all-start.7 = ((f32[2,32,8,256]{3,2,0,1:T(8,128)}), f32[2,32,8,256]{3,2,0,1:T(8,128)S(1)}, u32[]{:S(2)}, u32[]{:S(2)}) async-start(f32[2,32,8,256]{3,2,0,1:T(8,128)} %copy.248), calls=%async_computation.7 | async-start | bytes 1048576 | tf_op jit(solution)/shard_map/all_to_all | solution.py:108
  474.0 5.5 collective-permute-start.1
